TPU v7x, 32 devices: a whole 2x2x4 slice. The times are simulated.
32 devices in a mesh: region: 8 (over y, x, core), brick: 4 (over z).
Axes of the slice: x: 2, y: 2, z: 4, core: 2. Of those that a mesh axis runs over, the one named last changes fastest.
Arguments:
- velocity: float32 [3, 128, 64, 256], P(None, 'region', 'brick'), may hold values from -6 to 6
- viscosity: float32 [128, 64, 256], P('region', 'brick'), may hold values from 0.05 to 0.5
- marker_pos: float32 [3, 131072], P(None, ('region', 'brick')), as said below
- marker_force: float32 [3, 131072], P(None, ('region', 'brick')), may hold values from -240 to 240
- slot_lists: int32 [32, 8192], P(('region', 'brick')), may hold values from 0 to 16384, as said below
Outputs:
- predicted: float32 [3, 128, 64, 256], P(None, 'region', 'brick')
Inputs may be any that keep to these rules, and one draw needn't show every extreme that they name: `slot_lists`: each row lists, in increasing order, the indices within its region group's 16384 markers of the markers whose second coordinate lies in that brick's rows, then is padded with 16384; every marker of the group stands in exactly one row, and in every region group one row is full. `marker_pos`: the first coordinate of a marker lies 2 or more cells inside its region group's slab, the third 2 or more cells from the grid's ends, and the second within the rows of the brick whose slot row lists it.
All inputs are finite; a program needn't handle non-finite values.
Results may differ from a plain program's by a relative error of at most 0.00088.
Values sent between devices are 32-bit elements; how exact they have to be, the bound alone decides.
No kernel may reach another device: no remote copies, remote signals or barrier semaphores. Data moves between devices by JAX's collectives and lax.ppermute only.
A program may use at most 192 MiB of HBM per device.

v0:
```python
import jax
import jax.numpy as jnp
from jax import lax
from jax.sharding import PartitionSpec as P


def from_behind(x, axis, by):
    peers = lax.axis_size(axis)
    pairs = [(i, i + by) for i in range(peers) if 0 <= i + by < peers]
    return lax.ppermute(x, axis, pairs)


def extended_2(block, sides, width):
    for axis, dim in sides:
        count = lax.axis_size(axis)
        forward = [(i, i + 1) for i in range(count - 1)]
        backward = [(target, source) for source, target in forward]
        low = lax.ppermute(
            lax.slice_in_dim(block, block.shape[dim] - width, None, axis=dim), axis, forward
        )
        high = lax.ppermute(lax.slice_in_dim(block, 0, width, axis=dim), axis, backward)
        block = jnp.concatenate([low, block, high], axis=dim)
    return block


def kernel_weight(dist):
    return jnp.where(jnp.abs(dist) < 2.0, 0.25 * (1.0 + jnp.cos(0.5 * jnp.pi * dist)), 0.0)


def spread_rows(pos, force, row_low, rows, col_low, cols, depth):
    count = pos.shape[1]
    block = 1024
    x_centre = (col_low + jnp.arange(cols, dtype=jnp.int32)).astype(jnp.float32) + 0.5
    y_centre = (row_low + jnp.arange(rows, dtype=jnp.int32)).astype(jnp.float32) + 0.5
    z_centre = jnp.arange(depth, dtype=jnp.int32).astype(jnp.float32) + 0.5

    def one_block(turn, total):
        start = turn * block
        pos_part = lax.dynamic_slice_in_dim(pos, start, block, 1)
        force_part = lax.dynamic_slice_in_dim(force, start, block, 1)
        weight_x = kernel_weight(x_centre[:, None] - pos_part[0][None, :])
        weight_y = kernel_weight(y_centre[:, None] - pos_part[1][None, :])
        weight_z = kernel_weight(z_centre[None, :] - pos_part[2][:, None])
        factor = (
            force_part[:, None, None, :] * weight_x[None, :, None, :] * weight_y[None, None, :, :]
        )
        factor = factor.reshape(3 * cols * rows, block).astype(jnp.bfloat16)
        return total + jnp.dot(
            factor, weight_z.astype(jnp.bfloat16), preferred_element_type=jnp.float32
        )

    empty = jnp.zeros((3 * cols * rows, depth), jnp.float32)
    total = lax.fori_loop(0, count // block, one_block, empty)
    return total.reshape(3, cols, rows, depth)


def side(array, axis, offset):
    parts = [slice(1, -1), slice(1, -1), slice(1, -1)]
    size = array.shape[array.ndim - 3 + axis]
    parts[axis] = slice(1 + offset, size - 1 + offset)
    if array.ndim == 4:
        return array[:, parts[0], parts[1], parts[2]]
    return array[parts[0], parts[1], parts[2]]


def advance(padded, force_field):
    vel = padded[:3]
    visc = padded[3]
    speed = side(vel, 0, 0)
    visc_mid = side(visc, 0, 0)
    diffusion = jnp.zeros_like(speed)
    advection = jnp.zeros_like(speed)
    for axis in range(3):
        upper = side(vel, axis, 1)
        lower = side(vel, axis, -1)
        visc_up = side(visc, axis, 1)
        visc_dn = side(visc, axis, -1)
        diffusion = (
            diffusion
            + 0.5 * (visc_mid + visc_up) * (upper - speed)
            - 0.5 * (visc_mid + visc_dn) * (speed - lower)
        )
        advection = advection + speed[axis][None] * (upper - lower) * 0.5
    return speed + 0.1 * (diffusion - advection + force_field)


def body(velocity, viscosity, marker_pos, marker_force, slot_lists):
    cols, own_rows, depth = viscosity.shape
    region = lax.axis_index("region")
    brick = lax.axis_index("brick")
    own_slots = slot_lists[0]
    row_low = brick * own_rows - 2
    rows = own_rows + 4
    blank = jnp.zeros((3, own_slots.shape[0]), jnp.float32)
    start = jnp.int32(0)
    pos_piece = lax.all_gather(marker_pos, "brick", axis=1, tiled=True)
    force_piece = lax.all_gather(marker_force, "brick", axis=1, tiled=True)
    length = pos_piece.shape[1]
    inside = ((own_slots >= start) & (own_slots < start + length))[None, :]
    local = jnp.clip(own_slots, 0, length - 1)
    pos = jnp.where(inside, jnp.take(pos_piece, local, axis=1), blank)
    force = jnp.where(inside, jnp.take(force_piece, local, axis=1), blank)
    field = spread_rows(pos, force, row_low, rows, region * cols, cols, depth)
    upper_rim = field[:, :, own_rows + 2 :, :]
    lower_rim = field[:, :, :2, :]
    from_below = from_behind(upper_rim, "brick", 1)
    from_above = from_behind(lower_rim, "brick", -1)
    centre = field[:, :, 2 : own_rows + 2, :]
    centre = centre.at[:, :, :2, :].add(from_below)
    force_field = centre.at[:, :, own_rows - 2 :, :].add(from_above)
    stacked = jnp.concatenate([velocity, viscosity[None]], axis=0)
    extended = extended_2(stacked, (("region", 1), ("brick", 2)), 1)
    padded = jnp.pad(extended, ((0, 0), (0, 0), (0, 0), (1, 1)))
    return advance(padded, force_field)


def solution(mesh):
    placed = (
        P(None, "region", "brick", None),
        P("region", "brick", None),
        P(None, ("region", "brick")),
        P(None, ("region", "brick")),
        P(("region", "brick"), None),
    )
    return jax.shard_map(
        body,
        mesh=mesh,
        in_specs=placed,
        out_specs=P(None, "region", "brick", None),
        check_vma=False,
    )
```

profile of v0, /device:TPU:19, one launch (start us, length us, event | category | flops | bytes accessed | tf_op | source)
XLA Modules:
  0.0 469.4 jit_solution(8026704652510305181)
XLA Ops:
  3.2 137.8 %all_gather.6 = f32[3,16384]{0,1:T(8,128)} all-gather(f32[3,4096]{0,1:T(8,128)S(1)} %copy.10), channel_id=1, replica_groups=mesh['region'=8,'brick'=4] {'brick'}, dimensions={1}, use_global_device_ids=true | all-gather | bytes 245760 | tf_op jit(solution)/shard_map/all_gather | solution.py:97
  141.7 138.8 %all_gather.7 = f32[3,16384]{0,1:T(8,128)} all-gather(f32[3,4096]{0,1:T(8,128)S(1)} %copy.11), channel_id=1, replica_groups=mesh['region'=8,'brick'=4] {'brick'}, dimensions={1}, use_global_device_ids=true | all-gather | bytes 245760 | tf_op jit(solution)/shard_map/all_gather | solution.py:96
  280.4 31.2 %gather_fusion = f32[8192,3]{1,0:T(8,128)} fusion(f32[3,16384]{0,1:T(8,128)} %all_gather.6, s32[8192]{0:T(1024)S(1)} %fusion.44), kind=kCustom, calls=%fused_computation.clone | custom fusion | bytes 229376 | tf_op jit(solution)/shard_map/jit(_take)/gather | solution.py:102
  311.7 31.3 %gather_fusion.1 = f32[8192,3]{1,0:T(8,128)} fusion(f32[3,16384]{0,1:T(8,128)} %all_gather.7, s32[8192]{0:T(1024)S(1)} %fusion.44), kind=kCustom, calls=%fused_computation.1.clone | custom fusion | bytes 229376 | tf_op jit(solution)/shard_map/jit(_take)/gather | solution.py:101
  342.9 8.0 %bitcast_select_fusion = (f32[3,8192]{0,1:T(8,128)}, f32[3,8192]{0,1:T(8,128)}) fusion(f32[8192,3]{1,0:T(8,128)} %gather_fusion.1, pred[8192]{0:T(1024)(128)(4,1)S(1)} %compare_and_fusion, pred[8192]{0:T(1024)(128)(4,1)S(1)} %and_reduce_fusion, f32[8192,3]{1,0:T(8,128)} %gather_fusion), kind=kLoop, calls=%fused_computation.47 | loop fusion | flops 98304 | bytes 409600 | tf_op jit(solution)/shard_map/jit(_where)/select_n | solution.py:101
  350.9 2.8 copy.12
  353.8 2.9 copy.13
  356.6 79.9 %while.16 = (s32[]{:T(128)}, f32[960,256]{1,0:T(8,128)S(1)}, f32[3,8192]{1,0:T(4,128)S(1)}, f32[3,8192]{1,0:T(4,128)S(1)}, s32[]{:T(128)}, /*index=5*/s32[]{:T(1...) while((s32[]{:T(128)}, f32[960,256]{1,0:T(8,128)S(1)}, ...), condition=%wide.region_1.3_spmd.clone, body=%wide.region_0.2_spmd.clone.sunk | while | flops 508179072 | bytes 11381301 | solution.py:53
  358.3 2.0 convert_element_type.63
  360.3 6.2 %convolution_add_fusion.2 = f32[960,256]{1,0:T(8,128)S(1)} fusion(bf16[960,1024]{1,0:T(8,128)(2,1)} %convert_element_type.63, f32[960,256]{1,0:T(8,128)S(1)} %get-tuple-element.284, f32[1024]{0:T(1024)S(1)} %bitcast.34, f32[256]{0:T(256)S(1)} %convert_add_fusion.8, pred[]{:T(512)S(6)} %compare.35), kind=kOutput, calls=%fused_computation.8.clone.1 | convolution fusion | flops 505905152 | bytes 3937281 | tf_op jit(solution)/shard_map/while/body/eval_jaxpr/dot_general | solution.py:48
  370.3 6.2 %convolution_add_fusion.2 = f32[960,256]{1,0:T(8,128)S(1)} fusion(bf16[960,1024]{1,0:T(8,128)(2,1)} %convert_element_type.63, f32[960,256]{1,0:T(8,128)S(1)} %get-tuple-element.284, f32[1024]{0:T(1024)S(1)} %bitcast.34, f32[256]{0:T(256)S(1)} %convert_add_fusion.8, pred[]{:T(512)S(6)} %compare.35), kind=kOutput, calls=%fused_computation.8.clone.1 | convolution fusion | flops 505905152 | bytes 3937281 | tf_op jit(solution)/shard_map/while/body/eval_jaxpr/dot_general | solution.py:48
  380.3 6.3 %convolution_add_fusion.2 = f32[960,256]{1,0:T(8,128)S(1)} fusion(bf16[960,1024]{1,0:T(8,128)(2,1)} %convert_element_type.63, f32[960,256]{1,0:T(8,128)S(1)} %get-tuple-element.284, f32[1024]{0:T(1024)S(1)} %bitcast.34, f32[256]{0:T(256)S(1)} %convert_add_fusion.8, pred[]{:T(512)S(6)} %compare.35), kind=kOutput, calls=%fused_computation.8.clone.1 | convolution fusion | flops 505905152 | bytes 3937281 | tf_op jit(solution)/shard_map/while/body/eval_jaxpr/dot_general | solution.py:48
  390.3 6.2 %convolution_add_fusion.2 = f32[960,256]{1,0:T(8,128)S(1)} fusion(bf16[960,1024]{1,0:T(8,128)(2,1)} %convert_element_type.63, f32[960,256]{1,0:T(8,128)S(1)} %get-tuple-element.284, f32[1024]{0:T(1024)S(1)} %bitcast.34, f32[256]{0:T(256)S(1)} %convert_add_fusion.8, pred[]{:T(512)S(6)} %compare.35), kind=kOutput, calls=%fused_computation.8.clone.1 | convolution fusion | flops 505905152 | bytes 3937281 | tf_op jit(solution)/shard_map/while/body/eval_jaxpr/dot_general | solution.py:48
  400.3 6.3 %convolution_add_fusion.2 = f32[960,256]{1,0:T(8,128)S(1)} fusion(bf16[960,1024]{1,0:T(8,128)(2,1)} %convert_element_type.63, f32[960,256]{1,0:T(8,128)S(1)} %get-tuple-element.284, f32[1024]{0:T(1024)S(1)} %bitcast.34, f32[256]{0:T(256)S(1)} %convert_add_fusion.8, pred[]{:T(512)S(6)} %compare.35), kind=kOutput, calls=%fused_computation.8.clone.1 | convolution fusion | flops 505905152 | bytes 3937281 | tf_op jit(solution)/shard_map/while/body/eval_jaxpr/dot_general | solution.py:48
  410.3 6.3 %convolution_add_fusion.2 = f32[960,256]{1,0:T(8,128)S(1)} fusion(bf16[960,1024]{1,0:T(8,128)(2,1)} %convert_element_type.63, f32[960,256]{1,0:T(8,128)S(1)} %get-tuple-element.284, f32[1024]{0:T(1024)S(1)} %bitcast.34, f32[256]{0:T(256)S(1)} %convert_add_fusion.8, pred[]{:T(512)S(6)} %compare.35), kind=kOutput, calls=%fused_computation.8.clone.1 | convolution fusion | flops 505905152 | bytes 3937281 | tf_op jit(solution)/shard_map/while/body/eval_jaxpr/dot_general | solution.py:48
  420.3 6.2 %convolution_add_fusion.2 = f32[960,256]{1,0:T(8,128)S(1)} fusion(bf16[960,1024]{1,0:T(8,128)(2,1)} %convert_element_type.63, f32[960,256]{1,0:T(8,128)S(1)} %get-tuple-element.284, f32[1024]{0:T(1024)S(1)} %bitcast.34, f32[256]{0:T(256)S(1)} %convert_add_fusion.8, pred[]{:T(512)S(6)} %compare.35), kind=kOutput, calls=%fused_computation.8.clone.1 | convolution fusion | flops 505905152 | bytes 3937281 | tf_op jit(solution)/shard_map/while/body/eval_jaxpr/dot_general | solution.py:48
  430.3 6.3 %convolution_add_fusion.2 = f32[960,256]{1,0:T(8,128)S(1)} fusion(bf16[960,1024]{1,0:T(8,128)(2,1)} %convert_element_type.63, f32[960,256]{1,0:T(8,128)S(1)} %get-tuple-element.284, f32[1024]{0:T(1024)S(1)} %bitcast.34, f32[256]{0:T(256)S(1)} %convert_add_fusion.8, pred[]{:T(512)S(6)} %compare.35), kind=kOutput, calls=%fused_computation.8.clone.1 | convolution fusion | flops 505905152 | bytes 3937281 | tf_op jit(solution)/shard_map/while/body/eval_jaxpr/dot_general | solution.py:48
  436.8 4.9 %collective-permute-start.4 = (f32[3,16,2,256]{3,2,1,0:T(2,128)S(1)}, f32[3,16,2,256]{3,2,1,0:T(2,128)S(1)}, u32[]{:S(2)}, u32[]{:S(2)}) collective-permute-start(f32[3,16,2,256]{3,2,1,0:T(2,128)S(1)} %get-tuple-element.214), channel_id=1, source_target_pairs={{0,1},{1,2},{2,3},{4,5},{5,6},{6,7},{8,9},{9,10},{10,11},{12,13},{... | collective-permute-start | bytes 294920 | tf_op jit(solution)/shard_map/ppermute | solution.py:10
  443.7 5.7 %collective-permute-start = (f32[4,1,16,256]{3,2,1,0:T(8,128)S(1)}, f32[4,1,16,256]{3,2,1,0:T(8,128)S(1)}, u32[]{:S(2)}, u32[]{:S(2)}) collective-permute-start(f32[4,1,16,256]{3,2,1,0:T(8,128)S(1)} %get-tuple-element.215), channel_id=1, source_target_pairs={{0,4},{4,8},{8,12},{12,16},{16,20},{20,24},{24,28},{1,5},{5,9},{9,... | collective-permute-start | bytes 196616 | tf_op jit(solution)/shard_map/ppermute | solution.py:18
  451.4 4.4 collective-permute-done.1
  455.9 3.6 collective-permute-start.2
  459.6 2.1 collective-permute-start.3
  461.9 2.7 collective-permute-done.3
  466.6 2.8 multiply_add_fusion
  (141 shorter events, 37.4 us)
Async XLA Ops:
  3.2 137.8 %copy-start.4 = (f32[3,4096]{1,0:T(4,128)S(1)}, f32[3,4096]{1,0:T(4,128)}, u32[]{:S(2)}) copy-start(f32[3,4096]{1,0:T(4,128)} %param.15) | copy-start | bytes 147460
  356.6 0.7 copy-start.2
  360.3 6.3 %copy-start.3 = (f32[3,8192]{1,0:T(4,128)S(1)}, f32[3,8192]{1,0:T(4,128)}, u32[]{:S(2)}) copy-start(f32[3,8192]{1,0:T(4,128)} %copy-done.2) | copy-start | bytes 294916 | tf_op jit(solution)/shard_map/while
  366.6 0.7 copy-start.2
  370.3 6.3 %copy-start.3 = (f32[3,8192]{1,0:T(4,128)S(1)}, f32[3,8192]{1,0:T(4,128)}, u32[]{:S(2)}) copy-start(f32[3,8192]{1,0:T(4,128)} %copy-done.2) | copy-start | bytes 294916 | tf_op jit(solution)/shard_map/while
  380.3 6.3 %copy-start.3 = (f32[3,8192]{1,0:T(4,128)S(1)}, f32[3,8192]{1,0:T(4,128)}, u32[]{:S(2)}) copy-start(f32[3,8192]{1,0:T(4,128)} %copy-done.2) | copy-start | bytes 294916 | tf_op jit(solution)/shard_map/while
  386.6 0.7 copy-start.2
  390.3 6.3 %copy-start.3 = (f32[3,8192]{1,0:T(4,128)S(1)}, f32[3,8192]{1,0:T(4,128)}, u32[]{:S(2)}) copy-start(f32[3,8192]{1,0:T(4,128)} %copy-done.2) | copy-start | bytes 294916 | tf_op jit(solution)/shard_map/while
  396.6 0.7 copy-start.2
  400.3 6.3 %copy-start.3 = (f32[3,8192]{1,0:T(4,128)S(1)}, f32[3,8192]{1,0:T(4,128)}, u32[]{:S(2)}) copy-start(f32[3,8192]{1,0:T(4,128)} %copy-done.2) | copy-start | bytes 294916 | tf_op jit(solution)/shard_map/while
  406.6 0.7 copy-start.2
  410.3 6.3 %copy-start.3 = (f32[3,8192]{1,0:T(4,128)S(1)}, f32[3,8192]{1,0:T(4,128)}, u32[]{:S(2)}) copy-start(f32[3,8192]{1,0:T(4,128)} %copy-done.2) | copy-start | bytes 294916 | tf_op jit(solution)/shard_map/while
  416.6 0.7 copy-start.2
  420.3 6.3 %copy-start.3 = (f32[3,8192]{1,0:T(4,128)S(1)}, f32[3,8192]{1,0:T(4,128)}, u32[]{:S(2)}) copy-start(f32[3,8192]{1,0:T(4,128)} %copy-done.2) | copy-start | bytes 294916 | tf_op jit(solution)/shard_map/while
  426.6 0.7 copy-start.2
  430.3 6.3 %copy-start.3 = (f32[3,8192]{1,0:T(4,128)S(1)}, f32[3,8192]{1,0:T(4,128)}, u32[]{:S(2)}) copy-start(f32[3,8192]{1,0:T(4,128)} %copy-done.2) | copy-start | bytes 294916 | tf_op jit(solution)/shard_map/while
  436.6 7.1 %copy-start = (f32[3,16,16,256]{3,2,1,0:T(8,128)S(1)}, f32[3,16,16,256]{3,2,1,0:T(8,128)}, u32[]{:S(2)}) copy-start(f32[3,16,16,256]{3,2,1,0:T(8,128)} %param.13) | copy-start | bytes 2359300
  436.6 7.1 %copy-start.1 = (f32[16,16,256]{2,1,0:T(8,128)S(1)}, f32[16,16,256]{2,1,0:T(8,128)}, u32[]{:S(2)}) copy-start(f32[16,16,256]{2,1,0:T(8,128)} %param.14) | copy-start | bytes 786436
  436.8 24.9 %collective-permute-start.4 = (f32[3,16,2,256]{3,2,1,0:T(2,128)S(1)}, f32[3,16,2,256]{3,2,1,0:T(2,128)S(1)}, u32[]{:S(2)}, u32[]{:S(2)}) collective-permute-start(f32[3,16,2,256]{3,2,1,0:T(2,128)S(1)} %get-tuple-element.214), channel_id=1, source_target_pairs={{0,1},{1,2},{2,3},{4,5},{5,6},{6,7},{8,9},{9,10},{10,11},{12,13},{... | collective-permute-start | bytes 294920 | tf_op jit(solution)/shard_map/ppermute | solution.py:10
  441.7 20.1 %collective-permute-start.5 = (f32[3,16,2,256]{3,2,1,0:T(2,128)S(1)}, f32[3,16,2,256]{3,2,1,0:T(2,128)S(1)}, u32[]{:S(2)}, u32[]{:S(2)}) collective-permute-start(f32[3,16,2,256]{3,2,1,0:T(2,128)S(1)} %get-tuple-element.213), channel_id=1, source_target_pairs={{1,0},{2,1},{3,2},{5,4},{6,5},{7,6},{9,8},{10,9},{11,10},{13,12},{... | collective-permute-start | bytes 294920 | tf_op jit(solution)/shard_map/ppermute | solution.py:10
  443.7 7.8 %collective-permute-start = (f32[4,1,16,256]{3,2,1,0:T(8,128)S(1)}, f32[4,1,16,256]{3,2,1,0:T(8,128)S(1)}, u32[]{:S(2)}, u32[]{:S(2)}) collective-permute-start(f32[4,1,16,256]{3,2,1,0:T(8,128)S(1)} %get-tuple-element.215), channel_id=1, source_target_pairs={{0,4},{4,8},{8,12},{12,16},{16,20},{20,24},{24,28},{1,5},{5,9},{9,... | collective-permute-start | bytes 196616 | tf_op jit(solution)/shard_map/ppermute | solution.py:18
  449.3 6.5 %collective-permute-start.1 = (f32[4,1,16,256]{3,2,1,0:T(8,128)S(1)}, f32[4,1,16,256]{3,2,1,0:T(8,128)S(1)}, u32[]{:S(2)}, u32[]{:S(2)}) collective-permute-start(f32[4,1,16,256]{3,2,1,0:T(8,128)S(1)} %get-tuple-element.216), channel_id=1, source_target_pairs={{4,0},{8,4},{12,8},{16,12},{20,16},{24,20},{28,24},{5,1},{9,5},{13... | collective-permute-start | bytes 196616 | tf_op jit(solution)/shard_map/ppermute | solution.py:21
  455.9 6.0 %collective-permute-start.2 = (f32[4,18,1,256]{3,2,1,0:T(1,128)S(1)}, f32[4,18,1,256]{3,2,1,0:T(1,128)S(1)}, u32[]{:S(2)}, u32[]{:S(2)}) collective-permute-start(f32[4,18,1,256]{3,2,1,0:T(1,128)S(1)} %get-tuple-element.211), channel_id=1, source_target_pairs={{0,1},{1,2},{2,3},{4,5},{5,6},{6,7},{8,9},{9,10},{10,11},{12,13},{... | collective-permute-start | bytes 221192 | tf_op jit(solution)/shard_map/ppermute | solution.py:18
  459.6 5.1 %collective-permute-start.3 = (f32[4,18,1,256]{3,2,1,0:T(1,128)S(1)}, f32[4,18,1,256]{3,2,1,0:T(1,128)S(1)}, u32[]{:S(2)}, u32[]{:S(2)}) collective-permute-start(f32[4,18,1,256]{3,2,1,0:T(1,128)S(1)} %get-tuple-element.212), channel_id=1, source_target_pairs={{1,0},{2,1},{3,2},{5,4},{6,5},{7,6},{9,8},{10,9},{11,10},{13,12},{... | collective-permute-start | bytes 221192 | tf_op jit(solution)/shard_map/ppermute | solution.py:21
  (1 other events, 0.7 us)
where the time goes:
time: 470 us; the launch traced here: 469 us
  blocking collectives  277 us (59%)
  local copies, waits for them, and re-layouts  88.8 us (19%)
  matrix products  50 us (11%)
  other arithmetic  25.7 us (5%)
  starting transfers between devices  20.2 us (4%)
  waiting for transfers between devices  7.14 us (2%)
    all_gather x1, blocking collectives, body(): pos_piece = lax.all_gather(marker_pos, 'brick', axis=1, tiled=True)  139 us
    all_gather x1, blocking collectives, body(): force_piece = lax.all_gather(marker_force, 'brick', axis=1, tiled=True)  138 us
    dot_general x8, matrix products, one_block(): jnp.dot(factor, weight_z.astype(jnp.bfloat16), preferred_element_type=jnp...  50 us
    gather x1, local copies, waits for them, and re-layouts, body(): pos = jnp.where(inside, jnp.take(pos_piece, local, axis=1), blank)  31.3 us
    gather x1, local copies, waits for them, and re-layouts, body(): force = jnp.where(inside, jnp.take(force_piece, local, axis=1), blank)  31.2 us
    convert_element_type x8, local copies, waits for them, and re-layouts, one_block(): factor = factor.reshape(3 * cols * rows, block).astype(jnp.bfloat16)  16 us
  transfers between devices with their start and end apart: 6, of which 2 were waited for; matrix products, arithmetic and copies ran while one was open for 0% of the time, Pallas kernels for 0%

commit v1 on v0

--- a/solution.py
+++ b/solution.py
@@ -94,7 +94,14 @@
     blank = jnp.zeros((3, own_slots.shape[0]), jnp.float32)
     start = jnp.int32(0)
     pos_piece = lax.all_gather(marker_pos, "brick", axis=1, tiled=True)
-    force_piece = lax.all_gather(marker_force, "brick", axis=1, tiled=True)
+    ring = [marker_force]
+    for hop in range(3):
+        ring.append(lax.ppermute(ring[-1], "brick", [(dev, (dev + 1) % 4) for dev in range(4)]))
+    force_piece = jnp.roll(
+        jnp.concatenate(ring[::-1], axis=1),
+        (lax.axis_index("brick") + 1) * ring[0].shape[1],
+        axis=1,
+    )
     length = pos_piece.shape[1]
     inside = ((own_slots >= start) & (own_slots < start + length))[None, :]
     local = jnp.clip(own_slots, 0, length - 1)

time: 470 us -> 352 us (0.75)
  blocking collectives: 277 us -> 139 us
  local copies, waits for them, and re-layouts: 88.8 us -> 102 us
  matrix products: 50 us -> 57.3 us
    all_gather x1 -> x0, blocking collectives: 138 us -> none  [body(): force_piece = lax.all_gather(marker_force, 'brick', axis=1, tiled=True)]
    unnamed x10 -> x41, local copies, waits for them, and re-layouts: 7.83 us -> 16.5 us
    dot_general x8, matrix products: 50 us -> 57.3 us  [one_block(): jnp.dot(factor, weight_z.astype(jnp.bfloat16), preferred_element_type=jnp...]
    ppermute x2, waiting for transfers between devices: 7.13 us -> 0.78 us  [extended_2(): lax.ppermute(lax.slice_in_dim(block, 0, width, axis=dim), axis, backward)]
  transfers between devices with their start and end apart: 6 -> 9, of which waited for: 2 -> 2; matrix products, arithmetic and copies ran while one was open for 0% -> 11% of each run, Pallas kernels for 0% -> 0%
where the time goes in v1:
time: 352 us; the launch traced here: 348 us
  blocking collectives  139 us (39%)
  local copies, waits for them, and re-layouts  102 us (29%)
  matrix products  57.3 us (16%)
  other arithmetic  27.2 us (8%)
  starting transfers between devices  18.6 us (5%)
  waiting for transfers between devices  3.82 us (1%)
    all_gather x1, blocking collectives, body(): pos_piece = lax.all_gather(marker_pos, 'brick', axis=1, tiled=True)  139 us
    dot_general x8, matrix products, one_block(): jnp.dot(factor, weight_z.astype(jnp.bfloat16), preferred_element_type=jnp...  57.3 us
    gather x1, local copies, waits for them, and re-layouts, body(): pos = jnp.where(inside, jnp.take(pos_piece, local, axis=1), blank)  31.2 us
    gather x1, local copies, waits for them, and re-layouts, body(): force = jnp.where(inside, jnp.take(force_piece, local, axis=1), blank)  31.1 us
    unnamed x41, local copies, waits for them, and re-layouts  16.5 us
    convert_element_type x8, local copies, waits for them, and re-layouts, one_block(): factor = factor.reshape(3 * cols * rows, block).astype(jnp.bfloat16)  15.7 us
    select_n x1, other arithmetic, body(): pos = jnp.where(inside, jnp.take(pos_piece, local, axis=1), blank)  8.07 us
  transfers between devices with their start and end apart: 9, of which 2 were waited for; matrix products, arithmetic and copies ran while one was open for 11% of the time, Pallas kernels for 0%

profile of v1, /device:TPU:19, one launch (start us, length us, event | category | flops | bytes accessed | tf_op | source)
XLA Modules:
  0.0 347.9 jit_solution(15078338722081781222)
XLA Ops:
  2.9 3.9 %collective-permute-start = (f32[4,1,16,256]{3,2,1,0:T(8,128)}, f32[4,1,16,256]{3,2,1,0:T(8,128)S(1)}, u32[]{:S(2)}, u32[]{:S(2)}) collective-permute-start(f32[4,1,16,256]{3,2,1,0:T(8,128)} %get-tuple-element.221), channel_id=1, source_target_pairs={{0,4},{4,8},{8,12},{12,16},{16,20},{20,24},{24,28},{1,5},{5,9},{9,... | collective-permute-start | bytes 196616 | tf_op jit(solution)/shard_map/ppermute | solution.py:18
  9.6 2.0 slice_bitcast_fusion.3
  14.1 2.3 collective-permute-start.2
  16.4 2.9 collective-permute-start.3
  19.4 138.6 %all_gather.3 = f32[3,16384]{0,1:T(8,128)} all-gather(f32[3,4096]{0,1:T(8,128)S(1)} %copy.19), channel_id=1, replica_groups=mesh['region'=8,'brick'=4] {'brick'}, dimensions={1}, use_global_device_ids=true | all-gather | bytes 245760 | tf_op jit(solution)/shard_map/all_gather | solution.py:96
  157.9 31.2 %gather_fusion.1 = f32[8192,3]{1,0:T(8,128)} fusion(f32[3,16384]{0,1:T(8,128)} %all_gather.3, s32[8192]{0:T(1024)S(1)} %fusion.44), kind=kCustom, calls=%fused_computation.1.clone | custom fusion | bytes 229376 | tf_op jit(solution)/shard_map/jit(_take)/gather | solution.py:108
  197.0 5.1 %copy.22 = f32[3,16384]{0,1:T(8,128)} copy(f32[3,16384]{1,0:T(4,128)S(1)} %constant_dynamic-slice_fusion.2) | data formatting | bytes 393216
  202.1 31.1 %gather_fusion = f32[8192,3]{1,0:T(8,128)} fusion(f32[3,16384]{0,1:T(8,128)} %copy.22, s32[8192]{0:T(1024)S(1)} %fusion.44), kind=kCustom, calls=%fused_computation.clone | custom fusion | bytes 229376 | tf_op jit(solution)/shard_map/jit(_take)/gather | solution.py:109
  233.2 8.1 %bitcast_select_fusion = (f32[3,8192]{0,1:T(8,128)}, f32[3,8192]{0,1:T(8,128)}) fusion(f32[8192,3]{1,0:T(8,128)} %gather_fusion.1, pred[8192]{0:T(1024)(128)(4,1)S(1)} %compare_and_fusion, pred[8192]{0:T(1024)(128)(4,1)S(1)} %and_reduce_fusion, f32[8192,3]{1,0:T(8,128)} %gather_fusion), kind=kLoop, calls=%fused_computation.47 | loop fusion | flops 98304 | bytes 409600 | tf_op jit(solution)/shard_map/jit(_where)/select_n | solution.py:108
  241.3 2.8 copy.20
  244.1 2.9 copy.21
  247.0 87.1 %while.16 = (s32[]{:T(128)}, f32[960,256]{1,0:T(8,128)}, f32[3,8192]{1,0:T(4,128)S(1)}, f32[3,8192]{1,0:T(4,128)S(1)}, s32[]{:T(128)}, /*index=5*/s32[]{:T(128)}...) while((s32[]{:T(128)}, f32[960,256]{1,0:T(8,128)}, ...), condition=%wide.region_1.3_spmd.clone, body=%wide.region_0.2_spmd.clone.sunk | while | flops 508179072 | bytes 12167789 | solution.py:53
  250.7 6.9 %convolution_add_fusion.2 = f32[960,256]{1,0:T(8,128)} fusion(bf16[960,1024]{1,0:T(8,128)(2,1)} %convert_element_type.63, f32[960,256]{1,0:T(8,128)} %get-tuple-element.290, f32[1024]{0:T(1024)S(1)} %bitcast.34, f32[256]{0:T(256)S(1)} %convert_add_fusion.8, pred[]{:T(512)S(6)} %compare.36), kind=kOutput, calls=%fused_computation.8.clone.1 | convolution fusion | flops 505905152 | bytes 3937281 | tf_op jit(solution)/shard_map/while/body/eval_jaxpr/dot_general | solution.py:48
  261.4 7.2 %convolution_add_fusion.2 = f32[960,256]{1,0:T(8,128)} fusion(bf16[960,1024]{1,0:T(8,128)(2,1)} %convert_element_type.63, f32[960,256]{1,0:T(8,128)} %get-tuple-element.290, f32[1024]{0:T(1024)S(1)} %bitcast.34, f32[256]{0:T(256)S(1)} %convert_add_fusion.8, pred[]{:T(512)S(6)} %compare.36), kind=kOutput, calls=%fused_computation.8.clone.1 | convolution fusion | flops 505905152 | bytes 3937281 | tf_op jit(solution)/shard_map/while/body/eval_jaxpr/dot_general | solution.py:48
  272.3 7.2 %convolution_add_fusion.2 = f32[960,256]{1,0:T(8,128)} fusion(bf16[960,1024]{1,0:T(8,128)(2,1)} %convert_element_type.63, f32[960,256]{1,0:T(8,128)} %get-tuple-element.290, f32[1024]{0:T(1024)S(1)} %bitcast.34, f32[256]{0:T(256)S(1)} %convert_add_fusion.8, pred[]{:T(512)S(6)} %compare.36), kind=kOutput, calls=%fused_computation.8.clone.1 | convolution fusion | flops 505905152 | bytes 3937281 | tf_op jit(solution)/shard_map/while/body/eval_jaxpr/dot_general | solution.py:48
  283.2 7.2 %convolution_add_fusion.2 = f32[960,256]{1,0:T(8,128)} fusion(bf16[960,1024]{1,0:T(8,128)(2,1)} %convert_element_type.63, f32[960,256]{1,0:T(8,128)} %get-tuple-element.290, f32[1024]{0:T(1024)S(1)} %bitcast.34, f32[256]{0:T(256)S(1)} %convert_add_fusion.8, pred[]{:T(512)S(6)} %compare.36), kind=kOutput, calls=%fused_computation.8.clone.1 | convolution fusion | flops 505905152 | bytes 3937281 | tf_op jit(solution)/shard_map/while/body/eval_jaxpr/dot_general | solution.py:48
  294.1 7.2 %convolution_add_fusion.2 = f32[960,256]{1,0:T(8,128)} fusion(bf16[960,1024]{1,0:T(8,128)(2,1)} %convert_element_type.63, f32[960,256]{1,0:T(8,128)} %get-tuple-element.290, f32[1024]{0:T(1024)S(1)} %bitcast.34, f32[256]{0:T(256)S(1)} %convert_add_fusion.8, pred[]{:T(512)S(6)} %compare.36), kind=kOutput, calls=%fused_computation.8.clone.1 | convolution fusion | flops 505905152 | bytes 3937281 | tf_op jit(solution)/shard_map/while/body/eval_jaxpr/dot_general | solution.py:48
  305.0 7.2 %convolution_add_fusion.2 = f32[960,256]{1,0:T(8,128)} fusion(bf16[960,1024]{1,0:T(8,128)(2,1)} %convert_element_type.63, f32[960,256]{1,0:T(8,128)} %get-tuple-element.290, f32[1024]{0:T(1024)S(1)} %bitcast.34, f32[256]{0:T(256)S(1)} %convert_add_fusion.8, pred[]{:T(512)S(6)} %compare.36), kind=kOutput, calls=%fused_computation.8.clone.1 | convolution fusion | flops 505905152 | bytes 3937281 | tf_op jit(solution)/shard_map/while/body/eval_jaxpr/dot_general | solution.py:48
  316.0 7.2 %convolution_add_fusion.2 = f32[960,256]{1,0:T(8,128)} fusion(bf16[960,1024]{1,0:T(8,128)(2,1)} %convert_element_type.63, f32[960,256]{1,0:T(8,128)} %get-tuple-element.290, f32[1024]{0:T(1024)S(1)} %bitcast.34, f32[256]{0:T(256)S(1)} %convert_add_fusion.8, pred[]{:T(512)S(6)} %compare.36), kind=kOutput, calls=%fused_computation.8.clone.1 | convolution fusion | flops 505905152 | bytes 3937281 | tf_op jit(solution)/shard_map/while/body/eval_jaxpr/dot_general | solution.py:48
  326.9 7.2 %convolution_add_fusion.2 = f32[960,256]{1,0:T(8,128)} fusion(bf16[960,1024]{1,0:T(8,128)(2,1)} %convert_element_type.63, f32[960,256]{1,0:T(8,128)} %get-tuple-element.290, f32[1024]{0:T(1024)S(1)} %bitcast.34, f32[256]{0:T(256)S(1)} %convert_add_fusion.8, pred[]{:T(512)S(6)} %compare.36), kind=kOutput, calls=%fused_computation.8.clone.1 | convolution fusion | flops 505905152 | bytes 3937281 | tf_op jit(solution)/shard_map/while/body/eval_jaxpr/dot_general | solution.py:48
  335.6 3.3 collective-permute-start.7
  339.5 2.2 collective-permute-start.8
  341.8 3.0 collective-permute-done.8
  345.0 2.8 multiply_add_fusion
  (211 shorter events, 47.3 us)
Async XLA Ops:
  0.0 13.3 %copy-start.4 = (f32[16,16,256]{2,1,0:T(8,128)S(1)}, f32[16,16,256]{2,1,0:T(8,128)}, u32[]{:S(2)}) copy-start(f32[16,16,256]{2,1,0:T(8,128)} %param.14) | copy-start | bytes 786436
  0.0 13.3 %copy-start = (f32[3,16,16,256]{3,2,1,0:T(8,128)S(1)}, f32[3,16,16,256]{3,2,1,0:T(8,128)}, u32[]{:S(2)}) copy-start(f32[3,16,16,256]{3,2,1,0:T(8,128)} %param.13) | copy-start | bytes 2359300
  0.0 11.6 %copy-start.17 = (s32[1,8192]{1,0:T(1,128)S(1)}, s32[1,8192]{1,0:T(1,128)}, u32[]{:S(2)}) copy-start(s32[1,8192]{1,0:T(1,128)} %param.17) | copy-start | bytes 98308
  0.0 11.8 %copy-start.18 = (f32[3,4096]{1,0:T(4,128)S(1)}, f32[3,4096]{1,0:T(4,128)}, u32[]{:S(2)}) copy-start(f32[3,4096]{1,0:T(4,128)} %param.15) | copy-start | bytes 147460
  0.0 12.4 %collective-permute-start.4 = (f32[3,4096]{1,0:T(4,128)}, f32[3,4096]{1,0:T(4,128)}, u32[]{:S(2)}, u32[]{:S(2)}) collective-permute-start(f32[3,4096]{1,0:T(4,128)} %param.16), channel_id=1, source_target_pairs={{0,1},{1,2},{2,3},{3,0},{4,5},{5,6},{6,7},{7,4},{8,9},{9,10},{10,1... | collective-permute-start | bytes 147464 | tf_op jit(solution)/shard_map/ppermute | solution.py:99
  2.9 9.7 %collective-permute-start = (f32[4,1,16,256]{3,2,1,0:T(8,128)}, f32[4,1,16,256]{3,2,1,0:T(8,128)S(1)}, u32[]{:S(2)}, u32[]{:S(2)}) collective-permute-start(f32[4,1,16,256]{3,2,1,0:T(8,128)} %get-tuple-element.221), channel_id=1, source_target_pairs={{0,4},{4,8},{8,12},{12,16},{16,20},{20,24},{24,28},{1,5},{5,9},{9,... | collective-permute-start | bytes 196616 | tf_op jit(solution)/shard_map/ppermute | solution.py:18
  6.8 6.5 %collective-permute-start.1 = (f32[4,1,16,256]{3,2,1,0:T(8,128)S(1)}, f32[4,1,16,256]{3,2,1,0:T(8,128)S(1)}, u32[]{:S(2)}, u32[]{:S(2)}) collective-permute-start(f32[4,1,16,256]{3,2,1,0:T(8,128)S(1)} %get-tuple-element.222), channel_id=1, source_target_pairs={{4,0},{8,4},{12,8},{16,12},{20,16},{24,20},{28,24},{5,1},{9,5},{13... | collective-permute-start | bytes 196616 | tf_op jit(solution)/shard_map/ppermute | solution.py:21
  12.4 176.6 %collective-permute-start.5 = (f32[3,4096]{1,0:T(4,128)}, f32[3,4096]{1,0:T(4,128)}, u32[]{:S(2)}, u32[]{:S(2)}) collective-permute-start(f32[3,4096]{1,0:T(4,128)} %collective-permute-done.4), channel_id=1, source_target_pairs={{0,1},{1,2},{2,3},{3,0},{4,5},{5,6},{6,7},{7,4},{8,9},{9,10},{10,1... | collective-permute-start | bytes 147464 | tf_op jit(solution)/shard_map/ppermute | solution.py:99
  14.1 175.5 %collective-permute-start.2 = (f32[4,18,1,256]{3,2,1,0:T(1,128)}, f32[4,18,1,256]{3,2,1,0:T(1,128)S(1)}, u32[]{:S(2)}, u32[]{:S(2)}) collective-permute-start(f32[4,18,1,256]{3,2,1,0:T(1,128)} %get-tuple-element.217), channel_id=1, source_target_pairs={{0,1},{1,2},{2,3},{4,5},{5,6},{6,7},{8,9},{9,10},{10,11},{12,13},{... | collective-permute-start | bytes 221192 | tf_op jit(solution)/shard_map/ppermute | solution.py:18
  16.4 173.2 %collective-permute-start.3 = (f32[4,18,1,256]{3,2,1,0:T(1,128)}, f32[4,18,1,256]{3,2,1,0:T(1,128)S(1)}, u32[]{:S(2)}, u32[]{:S(2)}) collective-permute-start(f32[4,18,1,256]{3,2,1,0:T(1,128)} %get-tuple-element.218), channel_id=1, source_target_pairs={{1,0},{2,1},{3,2},{5,4},{6,5},{7,6},{9,8},{10,9},{11,10},{13,12},{... | collective-permute-start | bytes 221192 | tf_op jit(solution)/shard_map/ppermute | solution.py:21
  189.1 4.3 %collective-permute-start.6 = (f32[3,4096]{1,0:T(4,128)}, f32[3,4096]{1,0:T(4,128)S(1)}, u32[]{:S(2)}, u32[]{:S(2)}) collective-permute-start(f32[3,4096]{1,0:T(4,128)} %collective-permute-done.5), channel_id=1, source_target_pairs={{0,1},{1,2},{2,3},{3,0},{4,5},{5,6},{6,7},{7,4},{8,9},{9,10},{10,1... | collective-permute-start | bytes 147464 | tf_op jit(solution)/shard_map/ppermute | solution.py:99
  261.4 7.2 %copy-start.9 = (f32[3,8192]{1,0:T(4,128)S(1)}, f32[3,8192]{1,0:T(4,128)}, u32[]{:S(2)}) copy-start(f32[3,8192]{1,0:T(4,128)} %copy-done.8) | copy-start | bytes 294916 | tf_op jit(solution)/shard_map/while
  261.4 7.2 %copy-start.15 = (f32[3,8192]{1,0:T(4,128)S(1)}, f32[3,8192]{1,0:T(4,128)}, u32[]{:S(2)}) copy-start(f32[3,8192]{1,0:T(4,128)} %copy-done.14) | copy-start | bytes 294916 | tf_op jit(solution)/shard_map/while
  272.3 7.2 %copy-start.9 = (f32[3,8192]{1,0:T(4,128)S(1)}, f32[3,8192]{1,0:T(4,128)}, u32[]{:S(2)}) copy-start(f32[3,8192]{1,0:T(4,128)} %copy-done.8) | copy-start | bytes 294916 | tf_op jit(solution)/shard_map/while
  272.3 7.2 %copy-start.15 = (f32[3,8192]{1,0:T(4,128)S(1)}, f32[3,8192]{1,0:T(4,128)}, u32[]{:S(2)}) copy-start(f32[3,8192]{1,0:T(4,128)} %copy-done.14) | copy-start | bytes 294916 | tf_op jit(solution)/shard_map/while
  315.9 7.2 %copy-start.15 = (f32[3,8192]{1,0:T(4,128)S(1)}, f32[3,8192]{1,0:T(4,128)}, u32[]{:S(2)}) copy-start(f32[3,8192]{1,0:T(4,128)} %copy-done.14) | copy-start | bytes 294916 | tf_op jit(solution)/shard_map/while
  335.5 9.5 %copy-start.3 = (f32[4,18,18,258]{3,2,1,0:T(8,128)S(1)}, f32[4,18,18,258]{3,2,1,0:T(8,128)}, u32[]{:S(2)}) copy-start(f32[4,18,18,258]{3,2,1,0:T(8,128)} %copy-done.2) | copy-start | bytes 4012420
  335.5 9.5 %copy-start.5 = (f32[16,16,256]{2,1,0:T(8,128)S(1)}, f32[16,16,256]{2,1,0:T(8,128)}, u32[]{:S(2)}) copy-start(f32[16,16,256]{2,1,0:T(8,128)} %get-tuple-element.223) | copy-start | bytes 786436
  335.5 9.5 %copy-start.6 = (f32[16,16,256]{2,1,0:T(8,128)S(1)}, f32[16,16,256]{2,1,0:T(8,128)}, u32[]{:S(2)}) copy-start(f32[16,16,256]{2,1,0:T(8,128)} %get-tuple-element.224) | copy-start | bytes 786436
  335.5 9.5 %copy-start.7 = (f32[16,16,256]{2,1,0:T(8,128)S(1)}, f32[16,16,256]{2,1,0:T(8,128)}, u32[]{:S(2)}) copy-start(f32[16,16,256]{2,1,0:T(8,128)} %get-tuple-element.225) | copy-start | bytes 786436
  335.6 9.5 %copy-start.11 = (f32[4,18,1,256]{3,2,1,0:T(1,128)S(1)}, f32[4,18,1,256]{3,2,1,0:T(1,128)}, u32[]{:S(2)}) copy-start(f32[4,18,1,256]{3,2,1,0:T(1,128)} %copy-done.10) | copy-start | bytes 221188
  335.6 9.5 %copy-start.13 = (f32[4,18,1,256]{3,2,1,0:T(1,128)S(1)}, f32[4,18,1,256]{3,2,1,0:T(1,128)}, u32[]{:S(2)}) copy-start(f32[4,18,1,256]{3,2,1,0:T(1,128)} %copy-done.12) | copy-start | bytes 221188
  335.6 6.2 %collective-permute-start.7 = (f32[3,16,2,256]{3,2,1,0:T(2,128)S(1)}, f32[3,16,2,256]{3,2,1,0:T(2,128)S(1)}, u32[]{:S(2)}, u32[]{:S(2)}) collective-permute-start(f32[3,16,2,256]{3,2,1,0:T(2,128)S(1)} %get-tuple-element.220), channel_id=1, source_target_pairs={{0,1},{1,2},{2,3},{4,5},{5,6},{6,7},{8,9},{9,10},{10,11},{12,13},{... | collective-permute-start | bytes 294920 | tf_op jit(solution)/shard_map/ppermute | solution.py:10
  339.5 5.4 %collective-permute-start.8 = (f32[3,16,2,256]{3,2,1,0:T(2,128)S(1)}, f32[3,16,2,256]{3,2,1,0:T(2,128)S(1)}, u32[]{:S(2)}, u32[]{:S(2)}) collective-permute-start(f32[3,16,2,256]{3,2,1,0:T(2,128)S(1)} %get-tuple-element.219), channel_id=1, source_target_pairs={{1,0},{2,1},{3,2},{5,4},{6,5},{7,6},{9,8},{10,9},{11,10},{13,12},{... | collective-permute-start | bytes 294920 | tf_op jit(solution)/shard_map/ppermute | solution.py:10
  (32 other events, 109.4 us)
